TPU v7x, 32 devices: a whole 2x2x4 slice. The times are simulated.
32 devices in a mesh: dp: 16 (over z, x, core), tensor: 2 (over y).
Axes of the slice: x: 2, y: 2, z: 4, core: 2. Of those that a mesh axis runs over, the one named last changes fastest.
Arguments:
- layer_input: bfloat16 [16384, 1024], P('dp'), may hold values from -6 to 6
- segments: int32 [16, 1024], P('dp'), may hold values from 0 to 3, never falling along the last dimension, each value on 1 to 512 neighbouring positions
- expert_choice: int32 [16384, 2], P('dp'), may hold values from 0 to 3, as said below
- dispatch_order: int32 [16, 2048], P('dp'), may hold values from 0 to 2047, each once within a row
- norm_gain_one: float32 [1024], replicated, may hold values from 0.5 to 1.5
- w_query: bfloat16 [1024, 1024], P(None, 'tensor'), may hold values from -0.1875 to 0.1875
- w_key: bfloat16 [1024, 512], P(None, 'tensor'), may hold values from -0.1875 to 0.1875
- w_value: bfloat16 [1024, 512], P(None, 'tensor'), may hold values from -0.1875 to 0.1875
- w_out: bfloat16 [1024, 1024], P('tensor'), may hold values from -1 to 1
- norm_gain_two: float32 [1024], replicated, may hold values from 0.5 to 1.5
- w_router: bfloat16 [1024, 4], replicated, may hold values from -0.125 to 0.125
- w_gate: bfloat16 [4, 1024, 512], P(None, None, 'tensor'), may hold values from -0.1875 to 0.1875
- w_up: bfloat16 [4, 1024, 512], P(None, None, 'tensor'), may hold values from -0.1875 to 0.1875
- w_down: bfloat16 [4, 512, 1024], P(None, 'tensor'), may hold values from -0.5 to 0.5
- out_grad: bfloat16 [16384, 1024], P('dp'), may hold values from -6 to 6
Outputs:
- layer_output: bfloat16 [16384, 1024], P('dp')
- input_grad: float32 [16384, 1024], P('dp')
- norm_gain_one_grad: float32 [1024], replicated
- w_query_grad: float32 [1024, 1024], P(None, 'tensor')
- w_key_grad: float32 [1024, 512], P(None, 'tensor')
- w_value_grad: float32 [1024, 512], P(None, 'tensor')
- w_out_grad: float32 [1024, 1024], P('tensor')
- norm_gain_two_grad: float32 [1024], replicated
- w_router_grad: float32 [1024, 4], replicated
- w_gate_grad: float32 [4, 1024, 512], P(None, None, 'tensor')
- w_up_grad: float32 [4, 1024, 512], P(None, None, 'tensor')
- w_down_grad: float32 [4, 512, 1024], P(None, 'tensor')
Inputs may be any that keep to these rules, and one draw needn't show every extreme that they name: `segments`: along each sequence the segment numbers never fall; a document has at most 512 tokens. `expert_choice`: each token names 2 different experts. In each sequence one expert is named by exactly 832 of its tokens, and each other expert by fewer. `dispatch_order`: each row is a permutation of the pair numbers t * 2 + k of one sequence.
All inputs are finite; a program needn't handle non-finite values.
Results may differ from a plain program's by a relative error of at most 0.014.
The roundings to bfloat16 on the way count: a program that leaves them out, or rounds other values in their place, can miss the bound.
Values sent between devices are 32-bit elements; how exact they have to be, the bound alone decides.
No kernel may reach another device: no remote copies, remote signals or barrier semaphores. Data moves between devices by JAX's collectives and lax.ppermute only.
A program may use at most 1.0625 GiB of HBM per device.

v0:
```python
import jax
import jax.numpy as jnp
from jax import lax
from jax.sharding import PartitionSpec as P

D = 1024
HEAD_DIM = 64
EXPERTS = 4
TOPK = 2
CAP = 640
norm_eps = 1e-05
masked_value = -1e30


def normalize(values):
    inverse = lax.rsqrt(jnp.mean(values * values, axis=-1, keepdims=True) + norm_eps)
    return (values * inverse, inverse)


def norm_back(grad_normed, normed, inverse, gain_vec):
    scaled = grad_normed * gain_vec
    mean_term = jnp.mean(scaled * normed, axis=-1, keepdims=True)
    return (inverse * (scaled - normed * mean_term), jnp.sum(grad_normed * normed, axis=0))


def softmax_last(values):
    peak_value = jnp.max(values, axis=-1, keepdims=True)
    raised = jnp.exp(values - peak_value)
    return raised / jnp.sum(raised, axis=-1, keepdims=True)


def dispatch_tables(choice_rows, order_row):
    pair_count = order_row.shape[0]
    pair_expert = choice_rows.reshape(-1)
    ordered = pair_expert[order_row]
    expert_ids = jnp.arange(EXPERTS, dtype=jnp.int32)
    one_hot = (ordered[:, None] == expert_ids[None, :]).astype(jnp.int32)
    earlier = jnp.sum((jnp.cumsum(one_hot, axis=0) - one_hot) * one_hot, axis=1)
    target = jnp.where(earlier < CAP, ordered * CAP + earlier, EXPERTS * CAP)
    pair_target = jnp.zeros((pair_count,), jnp.int32).at[order_row].set(target)
    pair_ids = jnp.arange(pair_count, dtype=jnp.int32)
    empty_token = choice_rows.shape[0]
    slot_token = (
        jnp.full((EXPERTS * CAP + 1,), empty_token, jnp.int32).at[pair_target].set(pair_ids // TOPK)
    )
    slot_pair = jnp.full((EXPERTS * CAP + 1,), pair_count, jnp.int32).at[pair_target].set(pair_ids)
    return (slot_token[: EXPERTS * CAP], slot_pair[: EXPERTS * CAP])


def block_scores(query_block, key_heads, seg_query, seg_keys, begin_row, score_scale):
    scores = (
        jnp.einsum("rkgd,ckd->kgrc", query_block, key_heads, preferred_element_type=jnp.float32)
        * score_scale
    )
    row_pos = begin_row + jnp.arange(query_block.shape[0], dtype=jnp.int32)
    col_pos = jnp.arange(key_heads.shape[0], dtype=jnp.int32)
    allowed = (seg_query[:, None] == seg_keys[None, :]) & (col_pos[None, :] <= row_pos[:, None])
    return jnp.where(allowed, scores, masked_value)


def pack_grads(parts_count, wide, tall, vectors):
    rows = jnp.concatenate(wide + tall + [jnp.stack(vectors)], axis=0)
    return jnp.pad(rows, ((0, -rows.shape[0] % (8 * parts_count)), (0, 0)))


def per_device(
    layer_input,
    segments,
    expert_choice,
    dispatch_order,
    norm_gain_one,
    w_query,
    w_key,
    w_value,
    w_out,
    norm_gain_two,
    w_router,
    w_gate,
    w_up,
    w_down,
    out_grad,
):
    length = layer_input.shape[0]
    score_scale = HEAD_DIM ** (-0.5)
    local_heads = w_query.shape[1] // HEAD_DIM
    local_kv = w_key.shape[1] // HEAD_DIM
    group_size = local_heads // local_kv
    block_rows = min(512, length)
    parts_count = lax.axis_size("dp")
    seg_ids = segments[0]
    residual = layer_input.astype(jnp.float32)
    normed_one, inverse_one = normalize(residual)
    input_one = (normed_one * norm_gain_one).astype(jnp.bfloat16)
    query_heads = (
        jnp.dot(input_one, w_query, preferred_element_type=jnp.float32)
        .astype(jnp.bfloat16)
        .reshape(length, local_kv, group_size, HEAD_DIM)
    )
    key_heads = (
        jnp.dot(input_one, w_key, preferred_element_type=jnp.float32)
        .astype(jnp.bfloat16)
        .reshape(length, local_kv, HEAD_DIM)
    )
    value_heads = (
        jnp.dot(input_one, w_value, preferred_element_type=jnp.float32)
        .astype(jnp.bfloat16)
        .reshape(length, local_kv, HEAD_DIM)
    )
    heads_out = []
    log_sums = []
    for begin_row in range(0, length, block_rows):
        finish = begin_row + block_rows
        scores = block_scores(
            query_heads[begin_row:finish],
            key_heads[:finish],
            seg_ids[begin_row:finish],
            seg_ids[:finish],
            begin_row,
            score_scale,
        )
        row_peak = jnp.max(scores, axis=-1, keepdims=True)
        raised = jnp.exp(scores - row_peak)
        row_total = jnp.sum(raised, axis=-1, keepdims=True)
        probs_low = (raised / row_total).astype(jnp.bfloat16)
        heads_out.append(
            jnp.einsum(
                "kgrc,ckd->rkgd",
                probs_low,
                value_heads[:finish],
                preferred_element_type=jnp.float32,
            ).astype(jnp.bfloat16)
        )
        log_sums.append(row_peak + jnp.log(row_total))
    attended = jnp.concatenate(heads_out, axis=0).reshape(length, local_heads * HEAD_DIM)
    attn_part = jnp.dot(attended, w_out, preferred_element_type=jnp.float32)
    attn_total = lax.psum(attn_part, "tensor")
    middle = residual + attn_total
    normed_two, inverse_two = normalize(middle)
    input_two = (normed_two * norm_gain_two).astype(jnp.bfloat16)
    logits = jnp.dot(input_two, w_router, preferred_element_type=jnp.float32)
    choice_hot = (
        expert_choice[:, :, None] == jnp.arange(EXPERTS, dtype=jnp.int32)[None, None, :]
    ).astype(jnp.float32)
    picked = jnp.sum(logits[:, None, :] * choice_hot, axis=-1)
    gating = softmax_last(picked)
    slot_token, slot_pair = dispatch_tables(expert_choice, dispatch_order[0])
    padded = jnp.concatenate([input_two, jnp.zeros((1, D), jnp.bfloat16)], axis=0)
    routed_rows = padded[slot_token].reshape(EXPERTS, CAP, D)
    pair_total = length * TOPK
    gate_flat = jnp.concatenate([gating.reshape(-1), jnp.zeros((1,), jnp.float32)])
    slot_weight = gate_flat[slot_pair]
    gate_proj = jnp.einsum("ecd,edf->ecf", routed_rows, w_gate, preferred_element_type=jnp.float32)
    up_proj = jnp.einsum("ecd,edf->ecf", routed_rows, w_up, preferred_element_type=jnp.float32)
    sigma_gate = jax.nn.sigmoid(gate_proj)
    activated = gate_proj * sigma_gate
    hidden = (activated * up_proj).astype(jnp.bfloat16)
    expert_part = jnp.einsum(
        "ecf,efd->ecd", hidden, w_down, preferred_element_type=jnp.float32
    ).reshape(EXPERTS * CAP, D)
    routed_part = (
        jnp.zeros((length + 1, D), jnp.float32)
        .at[slot_token]
        .add(slot_weight[:, None] * expert_part)[:length]
    )
    routed_total = lax.psum(routed_part, "tensor")
    block_out = (middle + routed_total).astype(jnp.bfloat16)
    grad_top = out_grad.astype(jnp.float32)
    grad_padded = jnp.concatenate([grad_top, jnp.zeros((1, D), jnp.float32)], axis=0)
    slot_grad = grad_padded[slot_token]
    grad_expert = (slot_weight[:, None] * slot_grad).astype(jnp.bfloat16).reshape(EXPERTS, CAP, D)
    gate_slot_part = jnp.sum(slot_grad * expert_part, axis=-1)
    gate_pair_part = (
        jnp.zeros((pair_total + 1,), jnp.float32)
        .at[slot_pair]
        .add(gate_slot_part)[:pair_total]
        .reshape(length, TOPK)
    )
    grad_hidden = jnp.einsum(
        "ecd,efd->ecf", grad_expert, w_down, preferred_element_type=jnp.float32
    )
    grad_wdown = jnp.einsum("ecf,ecd->efd", hidden, grad_expert, preferred_element_type=jnp.float32)
    grad_gate_proj = (
        grad_hidden * up_proj * sigma_gate * (1.0 + gate_proj * (1.0 - sigma_gate))
    ).astype(jnp.bfloat16)
    grad_up_proj = (grad_hidden * activated).astype(jnp.bfloat16)
    grad_wgate = jnp.einsum(
        "ecd,ecf->edf", routed_rows, grad_gate_proj, preferred_element_type=jnp.float32
    )
    grad_wup = jnp.einsum(
        "ecd,ecf->edf", routed_rows, grad_up_proj, preferred_element_type=jnp.float32
    )
    grad_rows = jnp.einsum(
        "ecf,edf->ecd", grad_gate_proj, w_gate, preferred_element_type=jnp.float32
    )
    grad_rows = (
        grad_rows
        + jnp.einsum("ecf,edf->ecd", grad_up_proj, w_up, preferred_element_type=jnp.float32)
    ).reshape(EXPERTS * CAP, D)
    routed_grad_part = (
        jnp.zeros((length + 1, D), jnp.float32).at[slot_token].add(grad_rows)[:length]
    )
    routed_grad, gate_pair_grad = lax.psum((routed_grad_part, gate_pair_part), "tensor")
    grad_picked = gating * (
        gate_pair_grad - jnp.sum(gating * gate_pair_grad, axis=-1, keepdims=True)
    )
    grad_logits = jnp.sum(grad_picked[:, :, None] * choice_hot, axis=1).astype(jnp.bfloat16)
    grad_router = jnp.einsum(
        "td,te->de", input_two, grad_logits, preferred_element_type=jnp.float32
    )
    grad_input_two = routed_grad + jnp.einsum(
        "te,de->td", grad_logits, w_router, preferred_element_type=jnp.float32
    )
    grad_middle_norm, grad_gain_two = norm_back(
        grad_input_two, normed_two, inverse_two, norm_gain_two
    )
    grad_middle = grad_top + grad_middle_norm
    grad_attn = grad_middle.astype(jnp.bfloat16)
    grad_wout = jnp.einsum("tn,td->nd", attended, grad_attn, preferred_element_type=jnp.float32)
    grad_heads = (
        jnp.einsum("td,nd->tn", grad_attn, w_out, preferred_element_type=jnp.float32)
        .astype(jnp.bfloat16)
        .reshape(length, local_kv, group_size, HEAD_DIM)
    )
    grad_keys_sum = jnp.zeros((length, local_kv, HEAD_DIM), jnp.float32)
    grad_values_sum = jnp.zeros((length, local_kv, HEAD_DIM), jnp.float32)
    grad_query_list = []
    for index_block, begin_row in enumerate(range(0, length, block_rows)):
        finish = begin_row + block_rows
        query_block = query_heads[begin_row:finish]
        scores = block_scores(
            query_block,
            key_heads[:finish],
            seg_ids[begin_row:finish],
            seg_ids[:finish],
            begin_row,
            score_scale,
        )
        probs_exact = jnp.exp(scores - log_sums[index_block])
        probs_low = probs_exact.astype(jnp.bfloat16)
        grad_out_block = grad_heads[begin_row:finish]
        grad_probs = jnp.einsum(
            "rkgd,ckd->kgrc",
            grad_out_block,
            value_heads[:finish],
            preferred_element_type=jnp.float32,
        )
        row_dot = jnp.sum(probs_exact * grad_probs, axis=-1, keepdims=True)
        grad_scores = (probs_exact * (grad_probs - row_dot)).astype(jnp.bfloat16)
        grad_query_list.append(
            (
                jnp.einsum(
                    "kgrc,ckd->rkgd",
                    grad_scores,
                    key_heads[:finish],
                    preferred_element_type=jnp.float32,
                )
                * score_scale
            ).astype(jnp.bfloat16)
        )
        grad_keys_sum = grad_keys_sum.at[:finish].add(
            jnp.einsum(
                "kgrc,rkgd->ckd", grad_scores, query_block, preferred_element_type=jnp.float32
            )
            * score_scale
        )
        grad_values_sum = grad_values_sum.at[:finish].add(
            jnp.einsum(
                "kgrc,rkgd->ckd", probs_low, grad_out_block, preferred_element_type=jnp.float32
            )
        )
    grad_query = jnp.concatenate(grad_query_list, axis=0).reshape(length, local_heads * HEAD_DIM)
    grad_keys = grad_keys_sum.astype(jnp.bfloat16).reshape(length, local_kv * HEAD_DIM)
    grad_values = grad_values_sum.astype(jnp.bfloat16).reshape(length, local_kv * HEAD_DIM)
    grad_wquery = jnp.einsum("td,tn->dn", input_one, grad_query, preferred_element_type=jnp.float32)
    grad_wkey = jnp.einsum("td,tn->dn", input_one, grad_keys, preferred_element_type=jnp.float32)
    grad_wvalue = jnp.einsum(
        "td,tn->dn", input_one, grad_values, preferred_element_type=jnp.float32
    )
    input_grad_part = jnp.einsum(
        "tn,dn->td", grad_query, w_query, preferred_element_type=jnp.float32
    )
    input_grad_part = input_grad_part + jnp.einsum(
        "tn,dn->td", grad_keys, w_key, preferred_element_type=jnp.float32
    )
    input_grad_part = input_grad_part + jnp.einsum(
        "tn,dn->td", grad_values, w_value, preferred_element_type=jnp.float32
    )
    input_grad_one = lax.psum(input_grad_part, "tensor")
    grad_resid_norm, grad_gain_one = norm_back(
        input_grad_one, normed_one, inverse_one, norm_gain_one
    )
    grad_input = grad_middle + grad_resid_norm
    gate_wide = jnp.concatenate([grad_wgate[e] for e in range(EXPERTS)], axis=1)
    up_wide = jnp.concatenate([grad_wup[e] for e in range(EXPERTS)], axis=1)
    qkv_wide = jnp.concatenate([grad_wquery, grad_wkey, grad_wvalue], axis=1)
    hidden_part = w_down.shape[1]
    down_rows = grad_wdown.reshape(EXPERTS * hidden_part, D)
    packed = pack_grads(
        parts_count,
        [gate_wide, up_wide, qkv_wide],
        [down_rows, grad_wout],
        [grad_gain_one, grad_gain_two] + [grad_router[:, e] for e in range(EXPERTS)],
    )
    shares = lax.psum_scatter(packed, "dp", scatter_dimension=0, tiled=True)
    total = lax.all_gather(shares, "dp", axis=0, tiled=True)
    split = [hidden_part * e for e in range(EXPERTS + 1)]
    sum_gate = jnp.stack([total[:D, split[e] : split[e + 1]] for e in range(EXPERTS)])
    sum_up = jnp.stack([total[D : 2 * D, split[e] : split[e + 1]] for e in range(EXPERTS)])
    q_cols = w_query.shape[1]
    kv_cols = w_key.shape[1]
    sum_query = total[2 * D : 3 * D, :q_cols]
    sum_key = total[2 * D : 3 * D, q_cols : q_cols + kv_cols]
    sum_value = total[2 * D : 3 * D, q_cols + kv_cols : q_cols + 2 * kv_cols]
    at = 3 * D
    sum_down = total[at : at + EXPERTS * hidden_part].reshape(w_down.shape)
    at += EXPERTS * hidden_part
    sum_out = total[at : at + w_out.shape[0]]
    at += w_out.shape[0]
    small = total[at : at + 2 + EXPERTS]
    return (
        block_out,
        grad_input,
        small[0],
        sum_query,
        sum_key,
        sum_value,
        sum_out,
        small[1],
        small[2 : 2 + EXPERTS].T,
        sum_gate,
        sum_up,
        sum_down,
    )


def solution(mesh):
    in_specs = (
        P("dp", None),
        P("dp", None),
        P("dp", None),
        P("dp", None),
        P(),
        P(None, "tensor"),
        P(None, "tensor"),
        P(None, "tensor"),
        P("tensor", None),
        P(),
        P(),
        P(None, None, "tensor"),
        P(None, None, "tensor"),
        P(None, "tensor", None),
        P("dp", None),
    )
    out_specs = (
        P("dp", None),
        P("dp", None),
        P(),
        P(None, "tensor"),
        P(None, "tensor"),
        P(None, "tensor"),
        P("tensor", None),
        P(),
        P(),
        P(None, None, "tensor"),
        P(None, None, "tensor"),
        P(None, "tensor", None),
    )
    return jax.shard_map(
        per_device, mesh=mesh, in_specs=in_specs, out_specs=out_specs, check_vma=False
    )
```

profile of v0, /device:TPU:0, one launch (start us, length us, event | category | flops | bytes accessed | tf_op | source)
XLA Modules:
  0.0 1043.2 jit_solution(16456109151212319496)
XLA Ops:
  7.3 2.2 fusion.24
  10.4 2.6 convolution_convert_fusion.2
  18.9 2.0 copy-done.2
  23.0 7.5 fusion.101
  30.5 8.0 fusion.3
  38.5 7.5 fusion.61
  47.1 3.3 fusion.103
  51.1 11.8 %gather_fusion = s32[2048]{0:T(1024)S(1)} fusion(s32[2048]{0:T(1024)S(1)} %reshape.323, s32[2048]{0:T(1024)S(1)} %broadcast_clamp_fusion), kind=kCustom, calls=%fused_computation | custom fusion | bytes 24576 | tf_op jit(solution)/shard_map/gather | solution.py:35
  64.6 8.0 scatter_custom_fusion
  72.7 8.1 scatter_custom_fusion.1
  80.8 8.1 scatter_custom_fusion.2
  88.9 4.1 concatenate.38
  93.0 14.6 %gather_fusion.3 = f32[2560,1024]{1,0:T(8,128)} fusion(f32[1025,1024]{1,0:T(8,128)} %concatenate.38, s32[3072]{0:T(1024)S(1)} %pad_clamp_fusion), kind=kCustom, calls=%fused_computation.3 | custom fusion | bytes 20981760 | tf_op jit(solution)/shard_map/gather | solution.py:169
  107.7 53.5 %all-reduce.10.cloned.1.call-done = f32[1024,1024]{1,0:T(8,128)} async-done(((f32[1024,1024]{1,0:T(8,128)}), f32[1024,1024]{1,0:T(8,128)}) %all-reduce.10.cloned.1.call-update) | async-done | bytes 4194320 | tf_op jit(solution)/shard_map/psum | solution.py:136
  161.2 3.5 multiply_reduce_fusion.3
  167.5 3.1 concatenate.37
  170.6 13.9 %gather_fusion.2 = bf16[2560,1024]{1,0:T(8,128)(2,1)} fusion(bf16[1025,1024]{1,0:T(8,128)(2,1)} %concatenate.37, s32[3072]{0:T(1024)S(1)} %pad_clamp_fusion), kind=kCustom, calls=%fused_computation.2 | custom fusion | bytes 10496000 | tf_op jit(solution)/shard_map/gather | solution.py:148
  184.5 4.8 fusion.105
  189.4 6.0 multiply_convert_fusion.4
  195.4 5.6 multiply_reduce_fusion
  201.1 15.1 %scatter_custom_fusion.5 = f32[2049]{0:T(1024)S(1)} fusion(s32[2560]{0:T(1024)S(1)} %compare_select_fusion.1, f32[2560]{0:T(1024)S(1)} %reshape.410, f32[]{:T(128)} %constant.163.clone.1), kind=kCustom, calls=%fused_computation.164 | custom fusion | flops 2560 | bytes 8200 | tf_op jit(solution)/shard_map/scatter-add | solution.py:175
  216.9 5.0 psum.38
  222.4 13.8 %gather_fusion.1 = f32[2560]{0:T(1024)S(1)} fusion(f32[2049]{0:T(1024)S(1)} %pad_maximum_fusion.7, s32[3072]{0:T(1024)S(1)} %pad_clamp_fusion.1), kind=kCustom, calls=%fused_computation.1 | custom fusion | bytes 30720 | tf_op jit(solution)/shard_map/gather | solution.py:151
  236.3 8.2 multiply_convert_fusion.2
  247.0 5.5 convolution_add_fusion
  252.5 25.5 %scatter_custom_fusion.4 = f32[1025,1024]{1,0:T(8,128)} fusion(s32[2560]{0:T(1024)S(1)} %compare_select_fusion.2, f32[2560,1024]{1,0:T(8,128)} %bitcast.263, f32[]{:T(128)} %constant.163.clone.1), kind=kCustom, calls=%fused_computation.74 | custom fusion | flops 2621440 | bytes 4198912 | tf_op jit(solution)/shard_map/scatter-add | solution.py:200
  278.0 4.8 slice.307
  282.9 8.7 bitcast_multiply_fusion.1
  291.6 25.6 %scatter_custom_fusion.3 = f32[1025,1024]{1,0:T(8,128)} fusion(s32[2560]{0:T(1024)S(1)} %compare_select_fusion.2, f32[2560,1024]{1,0:T(8,128)} %bitcast_multiply_fusion.1, f32[]{:T(128)} %constant.163.clone.1), kind=kCustom, calls=%fused_computation.76 | custom fusion | flops 2621440 | bytes 4198912 | tf_op jit(solution)/shard_map/scatter-add | solution.py:163
  317.2 4.8 slice.306
  322.0 68.8 %all-reduce.12.cloned.1.call-done = f32[1024,1024]{1,0:T(8,128)} async-done(((f32[1024,1024]{1,0:T(8,128)}), f32[1024,1024]{1,0:T(8,128)}) %all-reduce.12.cloned.1.call-update) | async-done | bytes 4194320 | tf_op jit(solution)/shard_map/psum | solution.py:202
  390.9 5.8 multiply_reduce_fusion.1
  396.6 1.8 multiply_add_fusion
  402.0 5.1 fusion.7
  407.1 4.8 fusion.9
  416.1 8.1 fusion
  424.2 2.8 fusion.46
  427.1 2.8 fusion.108
  429.8 8.5 fusion.2
  439.9 2.7 fusion.49
  445.8 3.3 add_add_fusion
  450.4 8.0 fusion.35
  458.4 5.5 copy.146
  468.5 4.3 fusion.109
  473.5 2.7 pad_maximum_fusion
  477.6 1.8 fusion.110
  480.1 2.6 pad_maximum_fusion.1
  486.9 2.5 pad_maximum_fusion.2
  491.0 2.6 fusion.63
  493.6 154.3 %all-reduce.14.cloned.1.call-done = (f32[1024,1024]{1,0:T(8,128)}, f32[1024,1024]{1,0:T(8,128)}) async-done(((f32[1024,1024]{1,0:T(8,128)}, f32[1024,1024]{1,0:T(8,128)}), (f32[1024,1024]{1,0:T(8,128)}, f32[1024,1024]{1,0:T(8,128)})) %all-reduce.14.cloned.1.call-update) | async-done | bytes 8388624 | tf_op jit(solution)/shard_map/psum | solution.py:165
  647.9 3.3 fusion.23
  652.2 21.8 %concatenate.43 = f32[4614,1024]{0,1:T(8,128)} concatenate(f32[1024,1024]{0,1:T(8,128)} %pad_maximum_fusion, f32[1024,1024]{0,1:T(8,128)} %pad_maximum_fusion.1, f32[1024,1024]{0,1:T(8,128)} %pad_maximum_fusion.2, f32[1024,1024]{0,1:T(8,128)} %copy.146, f32[512,1024]{0,1:T(8,128)} %fusion.63, f32[1,1024]{0,1:T(8,128)} %copy.119, f32[1,1024]{0,1:T(8,128)} %copy.120, ...), dimensions={0} | concatenate | bytes 37797888 | tf_op jit(solution)/shard_map/concatenate | solution.py:62
  674.0 19.5 %copy.149 = f32[4614,1024]{1,0:T(8,128)} copy(f32[4614,1024]{0,1:T(8,128)} %concatenate.43) | data formatting | bytes 37797888
  693.5 16.2 %pad.18.clone = f32[4736,1024]{1,0:T(8,128)} pad(f32[4614,1024]{1,0:T(8,128)} %copy.149, f32[]{:T(128)} %constant.163.clone.1), padding=0_122x0_0 | pad | bytes 38297604 | tf_op jit(solution)/shard_map/jit(_pad)/pad | solution.py:63
  709.8 199.3 %reduce-scatter.4.cloned.1.call-done = f32[296,1024]{1,0:T(8,128)} async-done(((f32[4736,1024]{1,0:T(8,128)}), f32[296,1024]{1,0:T(8,128)}) %reduce-scatter.4.cloned.1.call-update) | async-done | bytes 1212432 | tf_op jit(solution)/shard_map/reduce_scatter | solution.py:304
  909.2 5.7 add_convert_fusion
  915.9 2.7 fusion.22
  918.5 92.6 %all-gather.2.cloned.1.call-done = f32[4736,1024]{1,0:T(8,128)} async-done(((f32[296,1024]{1,0:T(8,128)}), f32[4736,1024]{1,0:T(8,128)}) %all-gather.2.cloned.1.call-update) | async-done | bytes 19398672 | tf_op jit(solution)/shard_map/all_gather | solution.py:305
  1011.2 6.6 slice_bitcast_fusion.3
  1017.7 2.3 pad_maximum_fusion.4
  1020.0 2.4 pad_maximum_fusion.3
  1025.2 3.2 slice.327
  1028.4 3.2 slice.324
  1031.6 4.8 slice.338
  (247 shorter events, 50.3 us)
Async XLA Ops:
  7.2 188.2 %copy-start = (bf16[4,256,1024]{2,1,0:T(8,128)(2,1)S(1)}, bf16[4,256,1024]{2,1,0:T(8,128)(2,1)}, u32[]{:S(2)}) copy-start(bf16[4,256,1024]{2,1,0:T(8,128)(2,1)} %param.40) | copy-start | bytes 6291460
  7.2 5.9 copy-start.64
  7.2 5.9 copy-start.51
  7.2 154.0 %all-reduce.10.cloned.1.call-start = ((), (), s32[]{:S(2)}) async-start(), calls=%async_computation.1 | async-start | bytes 8388608 | tf_op jit(solution)/shard_map/psum | solution.py:136
  7.3 5.9 copy-start.9
  9.5 4.6 copy-start.59
  13.1 9.9 copy-start.45
  13.1 3.0 copy-start.31
  14.1 24.4 %copy-start.43 = (bf16[1024,256]{0,1:T(8,128)(2,1)}, bf16[1024,256]{0,1:T(8,128)(2,1)S(1)}, u32[]{:S(2)}) copy-start(bf16[1024,256]{0,1:T(8,128)(2,1)S(1)} %convolution_convert_fusion.3) | copy-start | bytes 1572868
  14.6 4.3 copy-start.41
  16.1 6.8 copy-start.38
  17.7 3.2 copy-start.2
  38.5 8.6 copy-start.49
  47.1 3.4 copy-start.54
  50.4 340.4 %all-reduce.12.cloned.1.call-start = ((), (), s32[]{:S(2)}) async-start(), calls=%async_computation.2 | async-start | bytes 8388608 | tf_op jit(solution)/shard_map/psum | solution.py:202
  107.7 57.0 %copy-start.58 = (f32[1024]{0:T(1024)S(1)}, f32[1024]{0:T(1024)}, u32[]{:S(2)}) copy-start(f32[1024]{0:T(1024)} %param.36) | copy-start | bytes 12292
  164.7 2.7 copy-start.3
  184.5 4.8 copy-start.5
  184.5 10.9 %slice-start.6 = ((s8[10485760]{0:T(1024)(128)(4,1)}), s8[4194304]{0:T(1024)(128)(4,1)S(1)}, s32[]{:S(2)}) async-start(s8[10485760]{0:T(1024)(128)(4,1)} %bitcast.251), calls=%async_computation.12 | async-start | bytes 8388608
  189.4 6.0 copy-start.67
  189.4 6.0 slice-start.7
  189.4 6.0 slice-start.8
  195.4 5.7 copy-start.20
  236.3 8.2 copy-start.56
  236.3 8.2 copy-start.26
  244.5 2.5 copy-start.35
  282.8 365.0 %all-reduce.14.cloned.1.call-start = ((), (), s32[]{:S(2)}) async-start(), calls=%async_computation.5 | async-start | bytes 16777216 | tf_op jit(solution)/shard_map/psum | solution.py:165
  322.0 74.6 %copy-start.17 = (bf16[1024,1024]{1,0:T(8,128)(2,1)S(1)}, bf16[1024,1024]{1,0:T(8,128)(2,1)}, u32[]{:S(2)}) copy-start(bf16[1024,1024]{1,0:T(8,128)(2,1)} %param.41) | copy-start | bytes 6291460
  390.9 5.8 copy-start.4
  390.9 9.7 slice-start.4
  396.6 4.0 slice-start.5
  407.1 4.9 copy-start.19
  407.1 8.2 slice-start
  407.1 8.2 slice-start.1
  407.1 8.2 slice-start.2
  412.0 4.1 slice-start.3
  424.2 2.9 copy-start.52
  427.0 11.3 %copy-start.29 = (bf16[1024,4,64]{0,2,1:T(8,128)(2,1)}, bf16[1024,4,64]{0,2,1:T(8,128)(2,1)S(1)}, u32[]{:S(2)}) copy-start(bf16[1024,4,64]{0,2,1:T(8,128)(2,1)S(1)} %fusion.46) | copy-start | bytes 1572868
  427.0 2.8 copy-start.55
  429.8 8.5 copy-start.46
  439.9 2.7 copy-start.53
  442.6 6.5 copy-start.36
  442.6 2.9 copy-start.13
  442.6 3.2 copy-start.48
  443.9 5.2 copy-start.27
  449.2 460.0 %reduce-scatter.4.cloned.1.call-start = ((), (), s32[]{:S(2)}) async-start(), calls=%async_computation.4 | async-start | bytes 20611072 | tf_op jit(solution)/shard_map/reduce_scatter | solution.py:304
  458.4 5.5 copy-start.12
  463.9 4.6 copy-start.23
  472.9 3.3 slice-start.9
  473.5 3.7 slice-start.10
  473.5 4.1 copy-start.25
  480.0 2.7 copy-start.62
  480.0 3.7 copy-start.10
  480.0 3.7 copy-start.30
  480.0 3.7 copy-start.60
  480.1 3.7 copy-start.65
  486.8 3.8 copy-start.7
  486.9 4.1 copy-start.16
  493.6 158.6 %copy-start.33 = (f32[1,1024]{0,1:T(8,128)S(1)}, f32[1,1024]{0,1:T(8,128)}, u32[]{:S(2)}) copy-start(f32[1,1024]{0,1:T(8,128)} %copy.124) | copy-start | bytes 12292
  493.6 158.6 %copy-start.34 = (f32[1,1024]{0,1:T(8,128)S(1)}, f32[1,1024]{0,1:T(8,128)}, u32[]{:S(2)}) copy-start(f32[1,1024]{0,1:T(8,128)} %copy.123) | copy-start | bytes 12292
  709.8 301.4 %all-gather.2.cloned.1.call-start = ((), (), s32[]{:S(2)}) async-start(), calls=%async_computation.3 | async-start | bytes 20611072 | tf_op jit(solution)/shard_map/all_gather | solution.py:305
  909.2 5.7 copy-start.8
  909.2 6.7 copy-start.14
  1028.4 8.0 copy-start.1
  (20 other events, 31.7 us)
Sparse Core Ops, SparseCore 0:
  50.6 110.5 all-reduce.9
  282.9 107.8 all-reduce.11
  449.3 198.5 all-reduce.13
  709.9 199.1 reduce-scatter.3
  910.6 100.5 all-gather.1
where the time goes:
time: 1050 us; the launch traced here: 1040 us
  waiting for transfers between devices  569 us (54%)
  local copies, waits for them, and re-layouts  204 us (19%)
  other arithmetic  132 us (13%)
  matrix products  117 us (11%)
  between operations  15.3 us (1%)
    reduce_scatter x1, waiting for transfers between devices, per_device(): shares = lax.psum_scatter(packed, 'dp', scatter_dimension=0, tiled=True)  199 us
    psum x1, waiting for transfers between devices, per_device(): routed_total = lax.psum(routed_part, 'tensor')  154 us
    all_gather x1, waiting for transfers between devices, per_device(): total = lax.all_gather(shares, 'dp', axis=0, tiled=True)  92.6 us
    psum x1, waiting for transfers between devices, per_device(): lax.psum((routed_grad_part, gate_pair_part), 'tensor')  68.8 us
    psum x1, waiting for transfers between devices, per_device(): attn_total = lax.psum(attn_part, 'tensor')  53.5 us
    unnamed x160, local copies, waits for them, and re-layouts  35.4 us
    scatter-add x1, other arithmetic, per_device(): routed_part = jnp.zeros((length + 1, D), jnp.float32).at[slot_token].add(...  25.6 us
    scatter-add x1, other arithmetic, per_device(): jnp.zeros((length + 1, D), jnp.float32).at[slot_token].add(grad_rows)  25.5 us
  transfers between devices with their start and end apart: 5, of which 5 were waited for; matrix products, arithmetic and copies ran while one was open for 14% of the time, Pallas kernels for 0%

commit v1 on v0

--- a/solution.py
+++ b/solution.py
@@ -10,6 +10,22 @@
 CAP = 640
 norm_eps = 1e-05
 masked_value = -1e30
+
+
+def ring_gather(x, axis, dim):
+    ways, here, step = (lax.axis_size(axis), lax.axis_index(axis), x.shape[dim])
+    lengths = [n * ways if d == dim else n for d, n in enumerate(x.shape)]
+    full = lax.dynamic_update_slice_in_dim(jnp.zeros(lengths, x.dtype), x, here * step, axis=dim)
+    going_up = going_down = x
+    for far in range(1, ways // 2 + 1):
+        going_up = lax.ppermute(going_up, axis, [(d, (d + 1) % ways) for d in range(ways)])
+        full = lax.dynamic_update_slice_in_dim(full, going_up, (here - far) % ways * step, axis=dim)
+        if 2 * far < ways:
+            going_down = lax.ppermute(going_down, axis, [(d, (d - 1) % ways) for d in range(ways)])
+            full = lax.dynamic_update_slice_in_dim(
+                full, going_down, (here + far) % ways * step, axis=dim
+            )
+    return full
 
 
 def normalize(values):
@@ -302,7 +318,7 @@
         [grad_gain_one, grad_gain_two] + [grad_router[:, e] for e in range(EXPERTS)],
     )
     shares = lax.psum_scatter(packed, "dp", scatter_dimension=0, tiled=True)
-    total = lax.all_gather(shares, "dp", axis=0, tiled=True)
+    total = ring_gather(shares, "dp", 0)
     split = [hidden_part * e for e in range(EXPERTS + 1)]
     sum_gate = jnp.stack([total[:D, split[e] : split[e + 1]] for e in range(EXPERTS)])
     sum_up = jnp.stack([total[D : 2 * D, split[e] : split[e + 1]] for e in range(EXPERTS)])

time: 1050 us -> 1170 us (1.11); the launches traced: 1040 us -> 1150 us
  starting transfers between devices: 0.21 us -> 133 us
  waiting for transfers between devices: 569 us -> 509 us
  local copies, waits for them, and re-layouts: 204 us -> 236 us
    ppermute x0 -> x15, starting transfers between devices: none -> 132 us  [the longest x8 128 us: ring_gather(): lax.ppermute(going_up, axis, [(d, (d + 1) % ways) for d in range(ways)])]
    all_gather x1 -> x0, waiting for transfers between devices: 92.6 us -> none  [per_device(): total = lax.all_gather(shares, 'dp', axis=0, tiled=True)]
    ppermute x0 -> x15, waiting for transfers between devices: none -> 33.3 us  [the longest x8 33.3 us: ring_gather(): lax.ppermute(going_up, axis, [(d, (d + 1) % ways) for d in range(ways)])]
    dynamic_update_slice x0 -> x16, local copies, waits for them, and re-layouts: none -> 23.6 us  [the longest x8 11.8 us: ring_gather(): lax.dynamic_update_slice_in_dim(full, going_up, (here - far) % ways * ste...]
    unnamed x160 -> x186, local copies, waits for them, and re-layouts: 35.4 us -> 34.6 us
  transfers between devices with their start and end apart: 5 -> 19, of which waited for: 5 -> 10; matrix products, arithmetic and copies ran while one was open for 14% -> 15% of each run, Pallas kernels for 0% -> 0%
where the time goes in v1:
time: 1170 us; the launch traced here: 1150 us
  waiting for transfers between devices  509 us (44%)
  local copies, waits for them, and re-layouts  236 us (20%)
  starting transfers between devices  133 us (11%)
  other arithmetic  131 us (11%)
  matrix products  118 us (10%)
  between operations  15.3 us (1%)
    reduce_scatter x1, waiting for transfers between devices, per_device(): shares = lax.psum_scatter(packed, 'dp', scatter_dimension=0, tiled=True)  199 us
    psum x1, waiting for transfers between devices, per_device(): routed_total = lax.psum(routed_part, 'tensor')  154 us
    ppermute x8, starting transfers between devices, ring_gather(): lax.ppermute(going_up, axis, [(d, (d + 1) % ways) for d in range(ways)])  128 us
    psum x1, waiting for transfers between devices, per_device(): lax.psum((routed_grad_part, gate_pair_part), 'tensor')  68.8 us
    psum x1, waiting for transfers between devices, per_device(): attn_total = lax.psum(attn_part, 'tensor')  53.5 us
    unnamed x186, local copies, waits for them, and re-layouts  34.6 us
    ppermute x8, waiting for transfers between devices, ring_gather(): lax.ppermute(going_up, axis, [(d, (d + 1) % ways) for d in range(ways)])  33.3 us
    scatter-add x1, other arithmetic, per_device(): routed_part = jnp.zeros((length + 1, D), jnp.float32).at[slot_token].add(...  25.6 us
  transfers between devices with their start and end apart: 19, of which 10 were waited for; matrix products, arithmetic and copies ran while one was open for 15% of the time, Pallas kernels for 0%

profile of v1, /device:TPU:0, one launch (start us, length us, event | category | flops | bytes accessed | tf_op | source)
XLA Modules:
  0.0 1147.4 jit_solution(995278441431053338)
XLA Ops:
  23.0 7.5 fusion.101
  30.5 8.0 fusion.3
  38.5 7.5 fusion.61
  47.1 3.3 fusion.103
  51.1 11.8 %gather_fusion = s32[2048]{0:T(1024)S(1)} fusion(s32[2048]{0:T(1024)S(1)} %reshape.323, s32[2048]{0:T(1024)S(1)} %broadcast_clamp_fusion), kind=kCustom, calls=%fused_computation | custom fusion | bytes 24576 | tf_op jit(solution)/shard_map/gather | solution.py:51
  64.7 8.0 scatter_custom_fusion
  72.7 8.1 scatter_custom_fusion.1
  80.8 8.1 scatter_custom_fusion.2
  88.9 4.1 concatenate.38
  93.0 14.6 %gather_fusion.3 = f32[2560,1024]{1,0:T(8,128)} fusion(f32[1025,1024]{1,0:T(8,128)} %concatenate.38, s32[3072]{0:T(1024)S(1)} %pad_clamp_fusion), kind=kCustom, calls=%fused_computation.3 | custom fusion | bytes 20981760 | tf_op jit(solution)/shard_map/gather | solution.py:185
  107.6 53.5 %all-reduce.10.cloned.1.call-done = f32[1024,1024]{1,0:T(8,128)} async-done(((f32[1024,1024]{1,0:T(8,128)}), f32[1024,1024]{1,0:T(8,128)}) %all-reduce.10.cloned.1.call-update) | async-done | bytes 4194320 | tf_op jit(solution)/shard_map/psum | solution.py:152
  161.2 3.5 multiply_reduce_fusion.3
  167.5 3.1 concatenate.37
  170.6 14.0 %gather_fusion.2 = bf16[2560,1024]{1,0:T(8,128)(2,1)} fusion(bf16[1025,1024]{1,0:T(8,128)(2,1)} %concatenate.37, s32[3072]{0:T(1024)S(1)} %pad_clamp_fusion), kind=kCustom, calls=%fused_computation.2 | custom fusion | bytes 10496000 | tf_op jit(solution)/shard_map/gather | solution.py:164
  184.6 4.8 fusion.105
  189.4 6.0 multiply_convert_fusion.4
  195.5 5.7 multiply_reduce_fusion
  201.1 15.1 %scatter_custom_fusion.5 = f32[2049]{0:T(1024)S(1)} fusion(s32[2560]{0:T(1024)S(1)} %compare_select_fusion.1, f32[2560]{0:T(1024)S(1)} %reshape.410, f32[]{:T(128)} %constant.251.clone.1), kind=kCustom, calls=%fused_computation.164 | custom fusion | flops 2560 | bytes 8200 | tf_op jit(solution)/shard_map/scatter-add | solution.py:191
  217.0 5.0 psum.38
  222.5 13.8 %gather_fusion.1 = f32[2560]{0:T(1024)S(1)} fusion(f32[2049]{0:T(1024)S(1)} %pad_maximum_fusion.7, s32[3072]{0:T(1024)S(1)} %pad_clamp_fusion.1), kind=kCustom, calls=%fused_computation.1 | custom fusion | bytes 30720 | tf_op jit(solution)/shard_map/gather | solution.py:167
  236.3 8.2 multiply_convert_fusion.2
  247.1 5.5 convolution_add_fusion
  252.6 25.5 %scatter_custom_fusion.4 = f32[1025,1024]{1,0:T(8,128)} fusion(s32[2560]{0:T(1024)S(1)} %compare_select_fusion.2, f32[2560,1024]{1,0:T(8,128)} %bitcast.263, f32[]{:T(128)} %constant.251.clone.1), kind=kCustom, calls=%fused_computation.74 | custom fusion | flops 2621440 | bytes 4198912 | tf_op jit(solution)/shard_map/scatter-add | solution.py:216
  278.1 4.8 slice.307
  283.0 8.7 bitcast_multiply_fusion.1
  291.7 25.6 %scatter_custom_fusion.3 = f32[1025,1024]{1,0:T(8,128)} fusion(s32[2560]{0:T(1024)S(1)} %compare_select_fusion.2, f32[2560,1024]{1,0:T(8,128)} %bitcast_multiply_fusion.1, f32[]{:T(128)} %constant.251.clone.1), kind=kCustom, calls=%fused_computation.76 | custom fusion | flops 2621440 | bytes 4198912 | tf_op jit(solution)/shard_map/scatter-add | solution.py:179
  317.3 4.8 slice.306
  322.1 68.8 %all-reduce.12.cloned.1.call-done = f32[1024,1024]{1,0:T(8,128)} async-done(((f32[1024,1024]{1,0:T(8,128)}), f32[1024,1024]{1,0:T(8,128)}) %all-reduce.12.cloned.1.call-update) | async-done | bytes 4194320 | tf_op jit(solution)/shard_map/psum | solution.py:218
  390.9 5.8 multiply_reduce_fusion.1
  402.1 5.1 fusion.7
  407.2 4.8 fusion.9
  416.2 8.2 fusion
  424.3 2.8 fusion.46
  427.2 2.8 fusion.108
  430.0 8.5 fusion.2
  440.1 2.6 fusion.49
  446.0 3.3 add_add_fusion
  450.6 7.9 fusion.35
  458.5 5.5 copy.166
  468.6 4.3 fusion.109
  473.6 2.7 pad_maximum_fusion
  493.7 154.3 %all-reduce.14.cloned.1.call-done = (f32[1024,1024]{1,0:T(8,128)}, f32[1024,1024]{1,0:T(8,128)}) async-done(((f32[1024,1024]{1,0:T(8,128)}, f32[1024,1024]{1,0:T(8,128)}), (f32[1024,1024]{1,0:T(8,128)}, f32[1024,1024]{1,0:T(8,128)})) %all-reduce.14.cloned.1.call-update) | async-done | bytes 8388624 | tf_op jit(solution)/shard_map/psum | solution.py:181
  648.0 3.3 fusion.23
  652.4 21.8 %concatenate.43 = f32[4614,1024]{0,1:T(8,128)} concatenate(f32[1024,1024]{0,1:T(8,128)} %pad_maximum_fusion, f32[1024,1024]{0,1:T(8,128)} %pad_maximum_fusion.1, f32[1024,1024]{0,1:T(8,128)} %pad_maximum_fusion.2, f32[1024,1024]{0,1:T(8,128)} %copy.166, f32[512,1024]{0,1:T(8,128)} %fusion.63, f32[1,1024]{0,1:T(8,128)} %copy.137, f32[1,1024]{0,1:T(8,128)} %copy.138, ...), dimensions={0} | concatenate | bytes 37797888 | tf_op jit(solution)/shard_map/concatenate | solution.py:78
  674.2 19.5 %copy.169 = f32[4614,1024]{1,0:T(8,128)} copy(f32[4614,1024]{0,1:T(8,128)} %concatenate.43) | data formatting | bytes 37797888
  693.7 16.2 %pad.18.clone = f32[4736,1024]{1,0:T(8,128)} pad(f32[4614,1024]{1,0:T(8,128)} %copy.169, f32[]{:T(128)} %constant.251.clone.1), padding=0_122x0_0 | pad | bytes 38297604 | tf_op jit(solution)/shard_map/jit(_pad)/pad | solution.py:79
  709.9 199.4 %reduce-scatter.4.cloned.1.call-done = f32[296,1024]{1,0:T(8,128)} async-done(((f32[4736,1024]{1,0:T(8,128)}), f32[296,1024]{1,0:T(8,128)}) %reduce-scatter.4.cloned.1.call-update) | async-done | bytes 1212432 | tf_op jit(solution)/shard_map/reduce_scatter | solution.py:320
  909.3 4.4 collective-permute-start.1
  913.7 14.6 %collective-permute-done = f32[296,1024]{1,0:T(8,128)S(1)} collective-permute-done((f32[296,1024]{1,0:T(8,128)}, f32[296,1024]{1,0:T(8,128)S(1)}, u32[]{:S(2)}, u32[]{:S(2)}) %collective-permute-start) | collective-permute-done | bytes 1212448 | tf_op jit(solution)/shard_map/ppermute | solution.py:21
  928.3 9.4 collective-permute-start.2
  937.7 9.4 collective-permute-done.2
  947.1 17.4 %collective-permute-start.4 = (f32[296,1024]{1,0:T(8,128)S(1)}, f32[296,1024]{1,0:T(8,128)S(1)}, u32[]{:S(2)}, u32[]{:S(2)}) collective-permute-start(f32[296,1024]{1,0:T(8,128)S(1)} %collective-permute-done.2), channel_id=1, source_target_pairs={{0,2},{2,4},{4,6},{6,8},{8,10},{10,12},{12,14},{14,16},{16,18},{18... | collective-permute-start | bytes 3637256 | tf_op jit(solution)/shard_map/ppermute | solution.py:21
  964.5 2.6 collective-permute-done.4
  967.1 25.9 %collective-permute-start.6 = (f32[296,1024]{1,0:T(8,128)S(1)}, f32[296,1024]{1,0:T(8,128)S(1)}, u32[]{:S(2)}, u32[]{:S(2)}) collective-permute-start(f32[296,1024]{1,0:T(8,128)S(1)} %collective-permute-done.4), channel_id=1, source_target_pairs={{0,2},{2,4},{4,6},{6,8},{8,10},{10,12},{12,14},{14,16},{16,18},{18... | collective-permute-start | bytes 3637256 | tf_op jit(solution)/shard_map/ppermute | solution.py:21
  995.5 24.6 %collective-permute-start.8 = (f32[296,1024]{1,0:T(8,128)S(1)}, f32[296,1024]{1,0:T(8,128)}, u32[]{:S(2)}, u32[]{:S(2)}) collective-permute-start(f32[296,1024]{1,0:T(8,128)S(1)} %collective-permute-done.6), channel_id=1, source_target_pairs={{0,2},{2,4},{4,6},{6,8},{8,10},{10,12},{12,14},{14,16},{16,18},{18... | collective-permute-start | bytes 3637256 | tf_op jit(solution)/shard_map/ppermute | solution.py:21
  1020.1 2.6 collective-permute-done.8
  1022.8 26.3 %collective-permute-start.10 = (f32[296,1024]{1,0:T(8,128)}, f32[296,1024]{1,0:T(8,128)}, u32[]{:S(2)}, u32[]{:S(2)}) collective-permute-start(f32[296,1024]{1,0:T(8,128)} %collective-permute-done.8), channel_id=1, source_target_pairs={{0,2},{2,4},{4,6},{6,8},{8,10},{10,12},{12,14},{14,16},{16,18},{18... | collective-permute-start | bytes 3637256 | tf_op jit(solution)/shard_map/ppermute | solution.py:21
  1049.2 5.5 fusion.22
  1054.7 21.8 %collective-permute-start.12 = (f32[296,1024]{1,0:T(8,128)}, f32[296,1024]{1,0:T(8,128)S(1)}, u32[]{:S(2)}, u32[]{:S(2)}) collective-permute-start(f32[296,1024]{1,0:T(8,128)} %collective-permute-done.10), channel_id=1, source_target_pairs={{0,2},{2,4},{4,6},{6,8},{8,10},{10,12},{12,14},{14,16},{16,18},{18... | collective-permute-start | bytes 3637256 | tf_op jit(solution)/shard_map/ppermute | solution.py:21
  1078.6 9.1 broadcast_in_dim.49
  1118.2 3.2 slice.327
  1121.3 3.1 slice.324
  1124.4 4.8 slice.338
  1129.2 6.5 slice_bitcast_fusion.3
  (317 shorter events, 104.7 us)
Async XLA Ops:
  7.2 188.3 %copy-start = (bf16[4,256,1024]{2,1,0:T(8,128)(2,1)S(1)}, bf16[4,256,1024]{2,1,0:T(8,128)(2,1)}, u32[]{:S(2)}) copy-start(bf16[4,256,1024]{2,1,0:T(8,128)(2,1)} %param.40) | copy-start | bytes 6291460
  7.2 5.9 copy-start.77
  7.2 5.9 copy-start.64
  7.2 154.0 %all-reduce.10.cloned.1.call-start = ((), (), s32[]{:S(2)}) async-start(), calls=%async_computation.1 | async-start | bytes 8388608 | tf_op jit(solution)/shard_map/psum | solution.py:152
  7.3 5.9 copy-start.9
  9.5 4.6 copy-start.72
  13.1 9.9 copy-start.58
  14.1 24.4 %copy-start.56 = (bf16[1024,256]{0,1:T(8,128)(2,1)}, bf16[1024,256]{0,1:T(8,128)(2,1)S(1)}, u32[]{:S(2)}) copy-start(bf16[1024,256]{0,1:T(8,128)(2,1)S(1)} %convolution_convert_fusion.3) | copy-start | bytes 1572868
  14.6 4.3 copy-start.41
  16.1 6.8 copy-start.38
  38.5 8.6 copy-start.62
  50.5 340.5 %all-reduce.12.cloned.1.call-start = ((), (), s32[]{:S(2)}) async-start(), calls=%async_computation.2 | async-start | bytes 8388608 | tf_op jit(solution)/shard_map/psum | solution.py:218
  107.6 57.1 %copy-start.71 = (f32[1024]{0:T(1024)S(1)}, f32[1024]{0:T(1024)}, u32[]{:S(2)}) copy-start(f32[1024]{0:T(1024)} %param.36) | copy-start | bytes 12292
  184.6 4.8 copy-start.6
  184.6 10.9 slice-start.6
  189.4 6.0 copy-start.80
  189.4 6.0 slice-start.7
  189.4 6.0 slice-start.8
  195.4 5.7 copy-start.19
  236.3 8.2 copy-start.69
  236.3 8.2 copy-start.25
  282.9 365.1 %all-reduce.14.cloned.1.call-start = ((), (), s32[]{:S(2)}) async-start(), calls=%async_computation.4 | async-start | bytes 16777216 | tf_op jit(solution)/shard_map/psum | solution.py:181
  322.1 74.6 %copy-start.16 = (bf16[1024,1024]{1,0:T(8,128)(2,1)S(1)}, bf16[1024,1024]{1,0:T(8,128)(2,1)}, u32[]{:S(2)}) copy-start(bf16[1024,1024]{1,0:T(8,128)(2,1)} %param.41) | copy-start | bytes 6291460
  390.9 5.8 copy-start.4
  390.9 9.7 slice-start.4
  407.2 4.9 copy-start.18
  407.2 8.2 slice-start
  407.2 8.2 slice-start.1
  407.2 8.2 slice-start.2
  427.2 11.3 copy-start.29
  430.0 8.5 copy-start.59
  442.7 6.5 copy-start.36
  444.1 5.2 copy-start.26
  449.3 460.0 %reduce-scatter.4.cloned.1.call-start = ((), (), s32[]{:S(2)}) async-start(), calls=%async_computation.3 | async-start | bytes 20611072 | tf_op jit(solution)/shard_map/reduce_scatter | solution.py:320
  458.5 5.5 copy-start.12
  464.1 4.6 copy-start.22
  493.7 158.7 %copy-start.33 = (f32[1,1024]{0,1:T(8,128)S(1)}, f32[1,1024]{0,1:T(8,128)}, u32[]{:S(2)}) copy-start(f32[1,1024]{0,1:T(8,128)} %copy.142) | copy-start | bytes 12292
  493.7 158.7 %copy-start.34 = (f32[1,1024]{0,1:T(8,128)S(1)}, f32[1,1024]{0,1:T(8,128)}, u32[]{:S(2)}) copy-start(f32[1,1024]{0,1:T(8,128)} %copy.141) | copy-start | bytes 12292
  909.3 19.0 %collective-permute-start = (f32[296,1024]{1,0:T(8,128)}, f32[296,1024]{1,0:T(8,128)S(1)}, u32[]{:S(2)}, u32[]{:S(2)}) collective-permute-start(f32[296,1024]{1,0:T(8,128)} %reduce-scatter.4.cloned.1.call-done), channel_id=1, source_target_pairs={{0,2},{2,4},{4,6},{6,8},{8,10},{10,12},{12,14},{14,16},{16,18},{18... | collective-permute-start | bytes 3637256 | tf_op jit(solution)/shard_map/ppermute | solution.py:21
  909.3 28.4 %collective-permute-start.1 = (f32[296,1024]{1,0:T(8,128)}, f32[296,1024]{1,0:T(8,128)S(1)}, u32[]{:S(2)}, u32[]{:S(2)}) collective-permute-start(f32[296,1024]{1,0:T(8,128)} %reduce-scatter.4.cloned.1.call-done), channel_id=1, source_target_pairs={{0,30},{2,0},{4,2},{6,4},{8,6},{10,8},{12,10},{14,12},{16,14},{18,... | collective-permute-start | bytes 3637256 | tf_op jit(solution)/shard_map/ppermute | solution.py:24
  928.3 91.8 %copy-start.44 = (f32[296,1024]{1,0:T(8,128)}, f32[296,1024]{1,0:T(8,128)S(1)}, u32[]{:S(2)}) copy-start(f32[296,1024]{1,0:T(8,128)S(1)} %collective-permute-done) | copy-start | bytes 3637252
  928.3 18.8 %collective-permute-start.2 = (f32[296,1024]{1,0:T(8,128)S(1)}, f32[296,1024]{1,0:T(8,128)S(1)}, u32[]{:S(2)}, u32[]{:S(2)}) collective-permute-start(f32[296,1024]{1,0:T(8,128)S(1)} %collective-permute-done), channel_id=1, source_target_pairs={{0,2},{2,4},{4,6},{6,8},{8,10},{10,12},{12,14},{14,16},{16,18},{18... | collective-permute-start | bytes 3637256 | tf_op jit(solution)/shard_map/ppermute | solution.py:21
  937.7 82.4 %copy-start.46 = (f32[296,1024]{1,0:T(8,128)}, f32[296,1024]{1,0:T(8,128)S(1)}, u32[]{:S(2)}) copy-start(f32[296,1024]{1,0:T(8,128)S(1)} %collective-permute-done.1) | copy-start | bytes 3637252
  937.7 26.7 %collective-permute-start.3 = (f32[296,1024]{1,0:T(8,128)S(1)}, f32[296,1024]{1,0:T(8,128)S(1)}, u32[]{:S(2)}, u32[]{:S(2)}) collective-permute-start(f32[296,1024]{1,0:T(8,128)S(1)} %collective-permute-done.1), channel_id=1, source_target_pairs={{0,30},{2,0},{4,2},{6,4},{8,6},{10,8},{12,10},{14,12},{16,14},{18,... | collective-permute-start | bytes 3637256 | tf_op jit(solution)/shard_map/ppermute | solution.py:24
  947.1 17.4 %copy-start.52 = (f32[296,1024]{1,0:T(8,128)}, f32[296,1024]{1,0:T(8,128)S(1)}, u32[]{:S(2)}) copy-start(f32[296,1024]{1,0:T(8,128)S(1)} %collective-permute-done.2) | copy-start | bytes 3637252
  947.1 20.0 %collective-permute-start.4 = (f32[296,1024]{1,0:T(8,128)S(1)}, f32[296,1024]{1,0:T(8,128)S(1)}, u32[]{:S(2)}, u32[]{:S(2)}) collective-permute-start(f32[296,1024]{1,0:T(8,128)S(1)} %collective-permute-done.2), channel_id=1, source_target_pairs={{0,2},{2,4},{4,6},{6,8},{8,10},{10,12},{12,14},{14,16},{16,18},{18... | collective-permute-start | bytes 3637256 | tf_op jit(solution)/shard_map/ppermute | solution.py:21
  964.4 84.6 %copy-start.54 = (f32[296,1024]{1,0:T(8,128)}, f32[296,1024]{1,0:T(8,128)S(1)}, u32[]{:S(2)}) copy-start(f32[296,1024]{1,0:T(8,128)S(1)} %collective-permute-done.3) | copy-start | bytes 3637252
  964.4 28.6 %collective-permute-start.5 = (f32[296,1024]{1,0:T(8,128)S(1)}, f32[296,1024]{1,0:T(8,128)S(1)}, u32[]{:S(2)}, u32[]{:S(2)}) collective-permute-start(f32[296,1024]{1,0:T(8,128)S(1)} %collective-permute-done.3), channel_id=1, source_target_pairs={{0,30},{2,0},{4,2},{6,4},{8,6},{10,8},{12,10},{14,12},{16,14},{18,... | collective-permute-start | bytes 3637256 | tf_op jit(solution)/shard_map/ppermute | solution.py:24
  967.1 82.0 %copy-start.50 = (f32[296,1024]{1,0:T(8,128)}, f32[296,1024]{1,0:T(8,128)S(1)}, u32[]{:S(2)}) copy-start(f32[296,1024]{1,0:T(8,128)S(1)} %collective-permute-done.4) | copy-start | bytes 3637252
  967.1 28.4 %collective-permute-start.6 = (f32[296,1024]{1,0:T(8,128)S(1)}, f32[296,1024]{1,0:T(8,128)S(1)}, u32[]{:S(2)}, u32[]{:S(2)}) collective-permute-start(f32[296,1024]{1,0:T(8,128)S(1)} %collective-permute-done.4), channel_id=1, source_target_pairs={{0,2},{2,4},{4,6},{6,8},{8,10},{10,12},{12,14},{14,16},{16,18},{18... | collective-permute-start | bytes 3637256 | tf_op jit(solution)/shard_map/ppermute | solution.py:21
  993.0 27.1 %collective-permute-start.7 = (f32[296,1024]{1,0:T(8,128)S(1)}, f32[296,1024]{1,0:T(8,128)}, u32[]{:S(2)}, u32[]{:S(2)}) collective-permute-start(f32[296,1024]{1,0:T(8,128)S(1)} %collective-permute-done.5), channel_id=1, source_target_pairs={{0,30},{2,0},{4,2},{6,4},{8,6},{10,8},{12,10},{14,12},{16,14},{18,... | collective-permute-start | bytes 3637256 | tf_op jit(solution)/shard_map/ppermute | solution.py:24
  995.5 27.2 %copy-start.48 = (f32[296,1024]{1,0:T(8,128)}, f32[296,1024]{1,0:T(8,128)S(1)}, u32[]{:S(2)}) copy-start(f32[296,1024]{1,0:T(8,128)S(1)} %collective-permute-done.6) | copy-start | bytes 3637252
  995.5 27.2 %collective-permute-start.8 = (f32[296,1024]{1,0:T(8,128)S(1)}, f32[296,1024]{1,0:T(8,128)}, u32[]{:S(2)}, u32[]{:S(2)}) collective-permute-start(f32[296,1024]{1,0:T(8,128)S(1)} %collective-permute-done.6), channel_id=1, source_target_pairs={{0,2},{2,4},{4,6},{6,8},{8,10},{10,12},{12,14},{14,16},{16,18},{18... | collective-permute-start | bytes 3637256 | tf_op jit(solution)/shard_map/ppermute | solution.py:21
  1020.1 29.0 %collective-permute-start.9 = (f32[296,1024]{1,0:T(8,128)}, f32[296,1024]{1,0:T(8,128)}, u32[]{:S(2)}, u32[]{:S(2)}) collective-permute-start(f32[296,1024]{1,0:T(8,128)} %collective-permute-done.7), channel_id=1, source_target_pairs={{0,30},{2,0},{4,2},{6,4},{8,6},{10,8},{12,10},{14,12},{16,14},{18,... | collective-permute-start | bytes 3637256 | tf_op jit(solution)/shard_map/ppermute | solution.py:24
  1022.8 32.0 %collective-permute-start.10 = (f32[296,1024]{1,0:T(8,128)}, f32[296,1024]{1,0:T(8,128)}, u32[]{:S(2)}, u32[]{:S(2)}) collective-permute-start(f32[296,1024]{1,0:T(8,128)} %collective-permute-done.8), channel_id=1, source_target_pairs={{0,2},{2,4},{4,6},{6,8},{8,10},{10,12},{12,14},{14,16},{16,18},{18... | collective-permute-start | bytes 3637256 | tf_op jit(solution)/shard_map/ppermute | solution.py:21
  1049.1 27.4 %copy-start.5 = (f32[1024,1024]{1,0:T(8,128)S(1)}, f32[1024,1024]{1,0:T(8,128)}, u32[]{:S(2)}) copy-start(f32[1024,1024]{1,0:T(8,128)} %copy-done.3) | copy-start | bytes 12582916
  1049.1 27.4 %copy-start.28 = (f32[1024,1024]{1,0:T(8,128)S(1)}, f32[1024,1024]{1,0:T(8,128)}, u32[]{:S(2)}) copy-start(f32[1024,1024]{1,0:T(8,128)} %get-tuple-element.80) | copy-start | bytes 12582916
  1049.1 44.3 %collective-permute-start.11 = (f32[296,1024]{1,0:T(8,128)}, f32[296,1024]{1,0:T(8,128)S(1)}, u32[]{:S(2)}, u32[]{:S(2)}) collective-permute-start(f32[296,1024]{1,0:T(8,128)} %collective-permute-done.9), channel_id=1, source_target_pairs={{0,30},{2,0},{4,2},{6,4},{8,6},{10,8},{12,10},{14,12},{16,14},{18,... | collective-permute-start | bytes 3637256 | tf_op jit(solution)/shard_map/ppermute | solution.py:24
  1054.7 39.8 %collective-permute-start.12 = (f32[296,1024]{1,0:T(8,128)}, f32[296,1024]{1,0:T(8,128)S(1)}, u32[]{:S(2)}, u32[]{:S(2)}) collective-permute-start(f32[296,1024]{1,0:T(8,128)} %collective-permute-done.10), channel_id=1, source_target_pairs={{0,2},{2,4},{4,6},{6,8},{8,10},{10,12},{12,14},{14,16},{16,18},{18... | collective-permute-start | bytes 3637256 | tf_op jit(solution)/shard_map/ppermute | solution.py:21
  1078.6 9.1 copy-start.43
  1078.6 10.3 copy-start.45
  1092.3 5.9 copy-start.49
  1093.4 18.2 %collective-permute-start.13 = (f32[296,1024]{1,0:T(8,128)S(1)}, f32[296,1024]{1,0:T(8,128)S(1)}, u32[]{:S(2)}, u32[]{:S(2)}) collective-permute-start(f32[296,1024]{1,0:T(8,128)S(1)} %collective-permute-done.11), channel_id=1, source_target_pairs={{0,30},{2,0},{4,2},{6,4},{8,6},{10,8},{12,10},{14,12},{16,14},{18,... | collective-permute-start | bytes 3637256 | tf_op jit(solution)/shard_map/ppermute | solution.py:24
  1094.5 19.8 %collective-permute-start.14 = (f32[296,1024]{1,0:T(8,128)S(1)}, f32[296,1024]{1,0:T(8,128)S(1)}, u32[]{:S(2)}, u32[]{:S(2)}) collective-permute-start(f32[296,1024]{1,0:T(8,128)S(1)} %collective-permute-done.12), channel_id=1, source_target_pairs={{0,2},{2,4},{4,6},{6,8},{8,10},{10,12},{12,14},{14,16},{16,18},{18... | collective-permute-start | bytes 3637256 | tf_op jit(solution)/shard_map/ppermute | solution.py:21
  (47 other events, 120.6 us)
Sparse Core Ops, SparseCore 0:
  50.6 110.5 all-reduce.9
  283.0 107.8 all-reduce.11
  449.4 198.5 all-reduce.13
  710.1 199.1 reduce-scatter.3
